TPU v7x, 128 devices: a whole 4x4x4 slice. The times are simulated.
128 devices in a mesh: amp: 128 (over y, x, z, core).
Axes of the slice: x: 4, y: 4, z: 4, core: 2. Of those that a mesh axis runs over, the one named last changes fastest.
Arguments:
- state: float32 [2, 16777216], P(None, 'amp'), may hold values from -6 to 6
- costate: float32 [2, 16777216], P(None, 'amp'), may hold values from -6 to 6
- gates: float32 [3, 2, 128, 128], replicated, may hold values from -1 to 1, as said below
Outputs:
- state_out: float32 [2, 16777216], P(None, 'amp')
- costate_out: float32 [2, 16777216], P(None, 'amp')
- gradients: float32 [3, 2, 128, 128], replicated
Inputs may be any that keep to these rules, and one draw needn't show every extreme that they name: Each gates[l, 0] + i gates[l, 1] is a unitary matrix.
All inputs are finite; a program needn't handle non-finite values.
Results may differ from a plain program's by a relative error of at most 0.0001.
Values sent between devices are 32-bit elements; how exact they have to be, the bound alone decides.
A program may use at most 64 MiB of HBM per device.

v0:
```python
import math

import jax
import jax.numpy as jnp
from jax import lax
from jax.sharding import PartitionSpec as P


def swapped(value, axis, distance):
    mask = 2**distance
    pairs = [(source, source ^ mask) for source in range(lax.axis_size(axis))]
    return lax.ppermute(value, axis, pairs)


def undo_gate(field, gate_now):
    gate_real = gate_now[0]
    gate_imag = gate_now[1]
    high = lax.Precision.HIGHEST
    dims = (((0,), (0,)), ((), ()))

    def contract(matrix, operand):
        return lax.dot_general(
            matrix, operand, dims, precision=high, preferred_element_type=jnp.float32
        )

    new_real = contract(gate_real, field[0]) + contract(gate_imag, field[1])
    new_imag = contract(gate_real, field[1]) - contract(gate_imag, field[0])
    return jnp.stack([new_real, new_imag], axis=0)


def gate_gradient(adjoint, amplitudes):
    high = lax.Precision.HIGHEST
    both_dims = (((0, 2), (0, 2)), ((), ()))
    one_dims = (((1,), (1,)), ((), ()))
    grad_real = lax.dot_general(
        adjoint, amplitudes, both_dims, precision=high, preferred_element_type=jnp.float32
    )
    grad_imag = lax.dot_general(
        adjoint[1], amplitudes[0], one_dims, precision=high, preferred_element_type=jnp.float32
    ) - lax.dot_general(
        adjoint[0], amplitudes[1], one_dims, precision=high, preferred_element_type=jnp.float32
    )
    return jnp.stack([grad_real, grad_imag], axis=0)


def half_swap(arrays, dev_bit, gate_bit, mover):
    shape_now = arrays[0].shape
    outer_len = shape_now[1] >> gate_bit + 1
    inner_len = (1 << gate_bit) * shape_now[2]
    own_bit = lax.axis_index("amp") >> dev_bit & 1
    kept_list = []
    sent_list = []
    for field in arrays:
        reshaped = field.reshape(2, outer_len, 2, inner_len)
        kept_list.append(lax.dynamic_index_in_dim(reshaped, own_bit, 2, keepdims=False))
        sent_list.append(lax.dynamic_index_in_dim(reshaped, 1 - own_bit, 2, keepdims=False))
    received = mover((sent_list[0], sent_list[1]))
    results = []
    for kept_half, got_half in zip(kept_list, received):
        first = jnp.stack([kept_half, got_half], axis=2)
        second = jnp.stack([got_half, kept_half], axis=2)
        results.append(jnp.where(own_bit == 0, first, second).reshape(shape_now))
    return (results[0], results[1])


def on_device(state, costate, gates):
    gate_order = gates.shape[2]
    columns = state.shape[1] // gate_order
    devices = lax.axis_size("amp")
    device_bits = devices.bit_length() - 1
    gate_bits = gate_order.bit_length() - 1
    grad_scale = 1.0 / math.sqrt(devices * columns)
    amplitudes = state.reshape(2, gate_order, columns)
    adjoint = costate.reshape(2, gate_order, columns)
    top_bit = device_bits - 1
    gradient_list = []
    for layer_index in range(gates.shape[0]):
        amplitudes = undo_gate(amplitudes, gates[layer_index])
        term = gate_gradient(adjoint, amplitudes)
        gradient_list.append(lax.psum(term, "amp") * grad_scale)
        adjoint = undo_gate(adjoint, gates[layer_index])
        if layer_index + 1 < gates.shape[0]:
            if layer_index % 2 == 0:
                amplitudes, adjoint = half_swap(
                    (amplitudes, adjoint),
                    top_bit,
                    gate_bits - 1,
                    lambda parts: swapped(parts, "amp", top_bit),
                )
                amplitudes, adjoint = half_swap(
                    (amplitudes, adjoint), 0, gate_bits - 2, lambda parts: swapped(parts, "amp", 0)
                )
            else:
                for bit_index in range(device_bits):
                    amplitudes, adjoint = half_swap(
                        (amplitudes, adjoint),
                        bit_index,
                        bit_index,
                        lambda parts: swapped(parts, "amp", bit_index),
                    )
    gradients = jnp.stack(gradient_list, axis=0)
    return (
        amplitudes.reshape(2, gate_order * columns),
        adjoint.reshape(2, gate_order * columns),
        gradients,
    )


def solution(mesh):
    return jax.shard_map(
        on_device,
        mesh=mesh,
        in_specs=(P(None, "amp"), P(None, "amp"), P()),
        out_specs=(P(None, "amp"), P(None, "amp"), P()),
        check_vma=False,
    )
```

profile of v0, /device:TPU:1, one launch (start us, length us, event | category | flops | bytes accessed | tf_op | source)
XLA Modules:
  0.0 430.6 jit_solution(6795114377779872578)
XLA Ops:
  7.2 8.9 %slice_reduce_fusion = (f32[131072]{0:T(1024)S(1)}, f32[131072]{0:T(1024)S(1)}, f32[131072]{0:T(1024)}, f32[131072]{0:T(1024)}) fusion(f32[2,131072]{1,0:T(2,128)} %param.4, f32[2,131072]{1,0:T(2,128)} %param.3), kind=kLoop, calls=%fused_computation.74 | loop fusion | bytes 4194304 | tf_op jit(solution)/shard_map/slice | solution.py:26
  20.8 3.0 dynamic-slice_reduce_fusion
  25.0 3.9 collective-permute-start.9
  33.7 2.2 dynamic-slice_reduce_fusion.1
  39.3 2.6 stack.371
  45.2 1.7 stack.372
  50.0 1.8 collective-permute-done
  51.8 1.7 stack.335
  56.1 2.0 collective-permute-start.1
  58.4 1.5 maximum_select_fusion.10
  63.3 1.5 maximum_select_fusion.1
  69.1 1.4 fusion.34
  74.1 3.6 constant_dynamic-slice_fusion.28
  78.8 1.5 squeeze.188
  80.9 1.4 fusion.3
  82.3 1.4 fusion.2
  83.8 2.2 stack.379
  91.9 1.6 convolution_bitcast_fusion.1
  93.6 1.5 stack.344
  95.0 1.5 maximum_select_fusion.2
  99.9 2.0 collective-permute-start.3
  104.0 1.5 maximum_select_fusion.11
  108.8 5.6 %collective-permute-done.3 = f32[2,32,2048]{2,1,0:T(8,128)} collective-permute-done((f32[2,32,2048]{2,1,0:T(8,128)}, f32[2,32,2048]{2,1,0:T(8,128)}, u32[]{:S(2)}, u32[]{:S(2)}) %collective-permute-start.3) | collective-permute-done | bytes 524320 | tf_op jit(solution)/shard_map/ppermute | solution.py:12
  115.8 1.6 maximum_select_fusion.3
  120.9 3.5 collective-permute-start.4
  127.0 1.6 maximum_select_fusion.12
  132.1 3.3 collective-permute-start.13
  135.4 4.6 %collective-permute-done.4 = f32[2,16,4096]{2,1,0:T(8,128)} collective-permute-done((f32[2,16,4096]{2,1,0:T(8,128)}, f32[2,16,4096]{2,1,0:T(8,128)}, u32[]{:S(2)}, u32[]{:S(2)}) %collective-permute-start.4) | collective-permute-done | bytes 524320 | tf_op jit(solution)/shard_map/ppermute | solution.py:12
  140.0 1.6 stack.350
  141.6 1.5 maximum_select_fusion.4
  148.0 3.3 collective-permute-done.13
  151.3 1.6 stack.387
  152.9 1.5 maximum_select_fusion.13
  159.2 1.6 stack.353
  160.8 1.5 maximum_select_fusion.5
  165.7 3.1 collective-permute-start.6
  168.8 2.3 collective-permute-done.14
  171.1 1.6 stack.390
  172.7 1.5 maximum_select_fusion.14
  177.6 2.8 collective-permute-start.15
  180.3 4.2 collective-permute-done.6
  184.5 1.4 stack.356
  185.9 1.5 maximum_select_fusion.6
  192.1 3.6 collective-permute-done.15
  197.2 1.5 maximum_select_fusion.15
  204.6 1.5 maximum_select_fusion.7
  207.4 7.2 %collective-permute-done.16 = f32[2,2,32768]{2,1,0:T(2,128)} collective-permute-done((f32[2,2,32768]{2,1,0:T(2,128)}, f32[2,2,32768]{2,1,0:T(2,128)}, u32[]{:S(2)}, u32[]{:S(2)}) %collective-permute-start.16) | collective-permute-done | bytes 524320 | tf_op jit(solution)/shard_map/ppermute | solution.py:12
  216.0 1.5 maximum_select_fusion.16
  219.8 2.8 collective-permute-start.17
  222.6 1.7 constant_dynamic-slice_fusion.16
  224.5 8.1 %collective-permute-done.17 = f32[2,1,65536]{2,1,0:T(1,128)S(1)} collective-permute-done((f32[2,1,65536]{2,1,0:T(1,128)S(1)}, f32[2,1,65536]{2,1,0:T(1,128)S(1)}, u32[]{:S(2)}, u32[]{:S(2)}) %collective-permute-start.17) | collective-permute-done | bytes 524320 | tf_op jit(solution)/shard_map/ppermute | solution.py:12
  232.6 1.5 maximum_select_fusion.17
  236.1 7.8 %collective-permute-done.8 = f32[2,1,65536]{2,1,0:T(1,128)} collective-permute-done((f32[2,1,65536]{2,1,0:T(1,128)}, f32[2,1,65536]{2,1,0:T(1,128)}, u32[]{:S(2)}, u32[]{:S(2)}) %collective-permute-start.8) | collective-permute-done | bytes 524320 | tf_op jit(solution)/shard_map/ppermute | solution.py:12
  243.9 2.8 maximum_select_fusion.8
  253.7 1.8 fusion.22
  255.5 1.6 fusion.87
  258.7 1.5 squeeze.197
  261.2 1.9 fusion.4
  263.1 1.8 fusion
  266.9 2.4 copy.53
  271.0 1.9 pad_maximum_fusion
  272.9 1.8 convolution_bitcast_fusion
  275.8 1.9 pad_maximum_fusion.1
  277.7 142.7 %all-reduce.3.cloned.1.call-done = (f32[2,128,128]{1,2,0:T(8,128)}, f32[2,128,128]{1,2,0:T(8,128)}, f32[2,128,128]{1,2,0:T(8,128)}) async-done(((f32[2,128,128]{1,2,0:T(8,128)}, f32[2,128,128]{1,2,0:T(8,128)}, f32[2,128,128]{1,2,0:T(8,128)}), (f32[2,128,128]{1,2,0:T(8,128)}, f32[2,128,128]{1,2,0:T(8,128)}, f32[2,128,128]{1,2,0:T(8,128)})) %all-reduce.3.cloned.1.call-update) | async-done | bytes 393232 | tf_op jit(solution)/shard_map/psum | solution.py:80
  (189 shorter events, 114.3 us)
Async XLA Ops:
  7.2 413.3 %all-reduce.3.cloned.1.call-start = ((), (), s32[]{:S(2)}) async-start(), calls=%async_computation | async-start | bytes 786432 | tf_op jit(solution)/shard_map/psum | solution.py:80
  16.2 1.0 copy-start
  23.8 5.2 %copy-start.15 = (f32[131072]{0:T(1024)S(1)}, f32[131072]{0:T(1024)}, u32[]{:S(2)}) copy-start(f32[131072]{0:T(1024)} %get-tuple-element.60) | copy-start | bytes 1572868
  25.0 20.2 %collective-permute-start.9 = (f32[2,1,65536]{2,0,1:T(2,128)}, f32[2,1,65536]{2,0,1:T(2,128)}, u32[]{:S(2)}, u32[]{:S(2)}) collective-permute-start(f32[2,1,65536]{2,0,1:T(2,128)} %bitcast.215), channel_id=1, source_target_pairs={{0,64},{1,65},{2,66},{3,67},{4,68},{5,69},{6,70},{7,71},{8,72},{9,... | collective-permute-start | bytes 1572872 | tf_op jit(solution)/shard_map/ppermute | solution.py:12
  28.9 1.0 copy-start.14
  37.0 14.7 %collective-permute-start = (f32[2,1,65536]{2,0,1:T(2,128)}, f32[2,1,65536]{2,0,1:T(2,128)}, u32[]{:S(2)}, u32[]{:S(2)}) collective-permute-start(f32[2,1,65536]{2,0,1:T(2,128)} %bitcast.223), channel_id=1, source_target_pairs={{0,64},{1,65},{2,66},{3,67},{4,68},{5,69},{6,70},{7,71},{8,72},{9,... | collective-permute-start | bytes 1572872 | tf_op jit(solution)/shard_map/ppermute | solution.py:12
  39.3 4.0 copy-start.1
  45.2 1.7 copy-start.2
  48.8 9.3 %collective-permute-start.10 = (f32[2,2,32768]{2,1,0:T(2,128)S(1)}, f32[2,2,32768]{2,1,0:T(2,128)S(1)}, u32[]{:S(2)}, u32[]{:S(2)}) collective-permute-start(f32[2,2,32768]{2,1,0:T(2,128)S(1)} %bitcast.244), channel_id=1, source_target_pairs={{0,1},{1,0},{2,3},{3,2},{4,5},{5,4},{6,7},{7,6},{8,9},{9,8},{10,11... | collective-permute-start | bytes 1572872 | tf_op jit(solution)/shard_map/ppermute | solution.py:12
  56.1 5.8 %collective-permute-start.1 = (f32[2,2,32768]{2,1,0:T(2,128)}, f32[2,2,32768]{2,1,0:T(2,128)}, u32[]{:S(2)}, u32[]{:S(2)}) collective-permute-start(f32[2,2,32768]{2,1,0:T(2,128)} %bitcast.222), channel_id=1, source_target_pairs={{0,1},{1,0},{2,3},{3,2},{4,5},{5,4},{6,7},{7,6},{8,9},{9,8},{10,11... | collective-permute-start | bytes 1572872 | tf_op jit(solution)/shard_map/ppermute | solution.py:12
  67.6 1.0 copy-start.9
  78.5 15.0 %collective-permute-start.2 = (f32[2,64,1024]{2,1,0:T(8,128)}, f32[2,64,1024]{2,1,0:T(8,128)}, u32[]{:S(2)}, u32[]{:S(2)}) collective-permute-start(f32[2,64,1024]{2,1,0:T(8,128)} %bitcast.221), channel_id=1, source_target_pairs={{0,1},{1,0},{2,3},{3,2},{4,5},{5,4},{6,7},{7,6},{8,9},{9,8},{10,11... | collective-permute-start | bytes 1572872 | tf_op jit(solution)/shard_map/ppermute | solution.py:12
  80.9 1.5 copy-start.3
  83.8 2.2 copy-start.6
  87.1 1.2 copy-start.8
  89.3 1.4 copy-start.16
  90.2 12.3 %collective-permute-start.11 = (f32[2,64,1024]{2,1,0:T(8,128)}, f32[2,64,1024]{2,1,0:T(8,128)}, u32[]{:S(2)}, u32[]{:S(2)}) collective-permute-start(f32[2,64,1024]{2,1,0:T(8,128)} %bitcast.213), channel_id=1, source_target_pairs={{0,1},{1,0},{2,3},{3,2},{4,5},{5,4},{6,7},{7,6},{8,9},{9,8},{10,11... | collective-permute-start | bytes 1572872 | tf_op jit(solution)/shard_map/ppermute | solution.py:12
  93.6 1.5 copy-start.7
  98.9 3.0 copy-start.18
  98.9 3.0 copy-start.19
  99.9 14.5 %collective-permute-start.3 = (f32[2,32,2048]{2,1,0:T(8,128)}, f32[2,32,2048]{2,1,0:T(8,128)}, u32[]{:S(2)}, u32[]{:S(2)}) collective-permute-start(f32[2,32,2048]{2,1,0:T(8,128)} %bitcast.220), channel_id=1, source_target_pairs={{0,2},{1,3},{2,0},{3,1},{4,6},{5,7},{6,4},{7,5},{8,10},{9,11},{10,... | collective-permute-start | bytes 1572872 | tf_op jit(solution)/shard_map/ppermute | solution.py:12
  108.8 16.8 %collective-permute-start.12 = (f32[2,32,2048]{2,1,0:T(8,128)}, f32[2,32,2048]{2,1,0:T(8,128)}, u32[]{:S(2)}, u32[]{:S(2)}) collective-permute-start(f32[2,32,2048]{2,1,0:T(8,128)} %bitcast.212), channel_id=1, source_target_pairs={{0,2},{1,3},{2,0},{3,1},{4,6},{5,7},{6,4},{7,5},{8,10},{9,11},{10,... | collective-permute-start | bytes 1572872 | tf_op jit(solution)/shard_map/ppermute | solution.py:12
  120.9 19.1 %collective-permute-start.4 = (f32[2,16,4096]{2,1,0:T(8,128)}, f32[2,16,4096]{2,1,0:T(8,128)}, u32[]{:S(2)}, u32[]{:S(2)}) collective-permute-start(f32[2,16,4096]{2,1,0:T(8,128)} %bitcast.219), channel_id=1, source_target_pairs={{0,4},{1,5},{2,6},{3,7},{4,0},{5,1},{6,2},{7,3},{8,12},{9,13},{10,... | collective-permute-start | bytes 1572872 | tf_op jit(solution)/shard_map/ppermute | solution.py:12
  132.1 19.1 %collective-permute-start.13 = (f32[2,16,4096]{2,1,0:T(8,128)}, f32[2,16,4096]{2,1,0:T(8,128)}, u32[]{:S(2)}, u32[]{:S(2)}) collective-permute-start(f32[2,16,4096]{2,1,0:T(8,128)} %bitcast.211), channel_id=1, source_target_pairs={{0,4},{1,5},{2,6},{3,7},{4,0},{5,1},{6,2},{7,3},{8,12},{9,13},{10,... | collective-permute-start | bytes 1572872 | tf_op jit(solution)/shard_map/ppermute | solution.py:12
  146.6 12.6 %collective-permute-start.5 = (f32[2,8,8192]{2,1,0:T(8,128)}, f32[2,8,8192]{2,1,0:T(8,128)}, u32[]{:S(2)}, u32[]{:S(2)}) collective-permute-start(f32[2,8,8192]{2,1,0:T(8,128)} %bitcast.218), channel_id=1, source_target_pairs={{0,8},{1,9},{2,10},{3,11},{4,12},{5,13},{6,14},{7,15},{8,0},{9,1},... | collective-permute-start | bytes 1572872 | tf_op jit(solution)/shard_map/ppermute | solution.py:12
  157.8 13.3 %collective-permute-start.14 = (f32[2,8,8192]{2,1,0:T(8,128)}, f32[2,8,8192]{2,1,0:T(8,128)}, u32[]{:S(2)}, u32[]{:S(2)}) collective-permute-start(f32[2,8,8192]{2,1,0:T(8,128)} %bitcast.210), channel_id=1, source_target_pairs={{0,8},{1,9},{2,10},{3,11},{4,12},{5,13},{6,14},{7,15},{8,0},{9,1},... | collective-permute-start | bytes 1572872 | tf_op jit(solution)/shard_map/ppermute | solution.py:12
  165.7 18.8 %collective-permute-start.6 = (f32[2,4,16384]{2,1,0:T(4,128)}, f32[2,4,16384]{2,1,0:T(4,128)}, u32[]{:S(2)}, u32[]{:S(2)}) collective-permute-start(f32[2,4,16384]{2,1,0:T(4,128)} %bitcast.217), channel_id=1, source_target_pairs={{0,16},{1,17},{2,18},{3,19},{4,20},{5,21},{6,22},{7,23},{8,24},{9,... | collective-permute-start | bytes 1572872 | tf_op jit(solution)/shard_map/ppermute | solution.py:12
  177.6 18.2 %collective-permute-start.15 = (f32[2,4,16384]{2,1,0:T(4,128)}, f32[2,4,16384]{2,1,0:T(4,128)}, u32[]{:S(2)}, u32[]{:S(2)}) collective-permute-start(f32[2,4,16384]{2,1,0:T(4,128)} %bitcast.209), channel_id=1, source_target_pairs={{0,16},{1,17},{2,18},{3,19},{4,20},{5,21},{6,22},{7,23},{8,24},{9,... | collective-permute-start | bytes 1572872 | tf_op jit(solution)/shard_map/ppermute | solution.py:12
  190.9 12.4 %collective-permute-start.7 = (f32[2,2,32768]{2,1,0:T(2,128)}, f32[2,2,32768]{2,1,0:T(2,128)}, u32[]{:S(2)}, u32[]{:S(2)}) collective-permute-start(f32[2,2,32768]{2,1,0:T(2,128)} %bitcast.216), channel_id=1, source_target_pairs={{0,32},{1,33},{2,34},{3,35},{4,36},{5,37},{6,38},{7,39},{8,40},{9,... | collective-permute-start | bytes 1572872 | tf_op jit(solution)/shard_map/ppermute | solution.py:12
  202.1 12.5 %collective-permute-start.16 = (f32[2,2,32768]{2,1,0:T(2,128)}, f32[2,2,32768]{2,1,0:T(2,128)}, u32[]{:S(2)}, u32[]{:S(2)}) collective-permute-start(f32[2,2,32768]{2,1,0:T(2,128)} %bitcast.208), channel_id=1, source_target_pairs={{0,32},{1,33},{2,34},{3,35},{4,36},{5,37},{6,38},{7,39},{8,40},{9,... | collective-permute-start | bytes 1572872 | tf_op jit(solution)/shard_map/ppermute | solution.py:12
  219.8 12.8 %collective-permute-start.17 = (f32[2,1,65536]{2,1,0:T(1,128)S(1)}, f32[2,1,65536]{2,1,0:T(1,128)S(1)}, u32[]{:S(2)}, u32[]{:S(2)}) collective-permute-start(f32[2,1,65536]{2,1,0:T(1,128)S(1)} %get-tuple-element.19), channel_id=1, source_target_pairs={{0,64},{1,65},{2,66},{3,67},{4,68},{5,69},{6,70},{7,71},{8,72},{9,... | collective-permute-start | bytes 1572872 | tf_op jit(solution)/shard_map/ppermute | solution.py:12
  224.3 19.6 %collective-permute-start.8 = (f32[2,1,65536]{2,1,0:T(1,128)}, f32[2,1,65536]{2,1,0:T(1,128)}, u32[]{:S(2)}, u32[]{:S(2)}) collective-permute-start(f32[2,1,65536]{2,1,0:T(1,128)} %get-tuple-element.41), channel_id=1, source_target_pairs={{0,64},{1,65},{2,66},{3,67},{4,68},{5,69},{6,70},{7,71},{8,72},{9,... | collective-permute-start | bytes 1572872 | tf_op jit(solution)/shard_map/ppermute | solution.py:12
  260.2 1.0 copy-start.17
  261.2 1.9 copy-start.4
  266.9 2.4 copy-start.5
  269.6 1.4 copy-start.10
  269.6 1.4 copy-start.13
  272.9 1.8 copy-start.20
  272.9 2.5 copy-start.12
  274.7 1.1 copy-start.11
  420.4 1.0 copy-start.22
  421.4 0.9 copy-start.21
Sparse Core Ops, SparseCore 0:
  275.5 144.8 all-reduce.2
where the time goes:
time: 439 us; the launch traced here: 431 us
  waiting for transfers between devices  193 us (44%)
  local copies, waits for them, and re-layouts  123 us (28%)
  matrix products  35.3 us (8%)
  other arithmetic  33.1 us (8%)
  starting transfers between devices  31 us (7%)
  between operations  15.5 us (4%)
    psum x1, waiting for transfers between devices, on_device(): gradient_list.append(lax.psum(term, 'amp') * grad_scale)  143 us
    ppermute x18, waiting for transfers between devices, swapped(): return lax.ppermute(value, axis, pairs)  49.9 us
    ppermute x18, starting transfers between devices, swapped(): return lax.ppermute(value, axis, pairs)  31 us
    unnamed x71, local copies, waits for them, and re-layouts  29.9 us
    select_n x18, other arithmetic, half_swap(): results.append(jnp.where(own_bit == 0, first, second).reshape(shape_now))  26.3 us
    another operation x18, local copies, waits for them, and re-layouts, half_swap(): first = jnp.stack([kept_half, got_half], axis=2)  26 us
    dynamic_slice x18, local copies, waits for them, and re-layouts, half_swap(): lax.dynamic_index_in_dim(reshaped, own_bit, 2, keepdims=False)  24.5 us
    dot_general x24, matrix products, contract(): lax.dot_general(matrix, operand, dims, precision=high, preferred_element_...  22.1 us
  transfers between devices with their start and end apart: 19, of which 13 were waited for; matrix products, arithmetic and copies ran while one was open for 27% of the time, Pallas kernels for 0%

commit v1 on v0

v1 whole, which is shorter than its diff:
```python
import functools
import math

import jax
import jax.numpy as jnp
from jax import lax
from jax.experimental import pallas as pl
from jax.experimental.pallas import tpu as pltpu
from jax.sharding import PartitionSpec as P

F32 = jnp.float32
BF16 = jnp.bfloat16
MESH = pl.DeviceIdType.MESH
K = 4
PLANE = 32
NT = (((1,), (1,)), ((), ()))


def split(value):
    high = value.astype(BF16)
    return high, (value - high.astype(F32)).astype(BF16)


def dot3(stacked, high, low, dims):
    rows = stacked.shape[0] // 2
    both = lax.dot_general(stacked, high, dims, preferred_element_type=F32)
    rest = lax.dot_general(stacked[:rows], low, dims, preferred_element_type=F32)
    return both[:rows] + (both[rows:] + rest)


def kernel(
    scale, psi_hbm, lam_hbm, gates_hbm, psi_out, lam_out, grad_out,
    psi_in, lam_in, gates, mats, s0, r1, s1, r2, r3, vh, vl, acc,
    psi_res, lam_res, terms, mr, yb, gout,
    in_sem, out_sem, swap_send, swap_recv, xz_send, xz_recv, y_send, y_recv, own_sem,
    rs_send, rs_recv, ye_send, ye_recv, ag_send, ag_recv,
):
    me = lax.axis_index("amp")
    y = me // PLANE
    m = lax.rem(me, PLANE)
    core = lax.rem(me, 2)
    y_high = y // 2
    y_low = lax.rem(y, 2)
    barrier = pltpu.get_barrier_semaphore()

    def remote(src, dst, send, recv, device):
        return pltpu.make_async_remote_copy(
            src_ref=src, dst_ref=dst, send_sem=send, recv_sem=recv,
            device_id=(device,), device_id_type=MESH,
        )

    def plane_peer(i):
        return lax.rem(m + i, PLANE)

    def swap_dest(j):
        return (2 * (j // 2) + 1 - y_low) * PLANE + (m - core) + j % 2

    def greet(i, carry):
        pl.semaphore_signal(
            barrier, inc=1, device_id=(y * PLANE + plane_peer(i),), device_id_type=MESH
        )
        return carry

    loads = [
        pltpu.make_async_copy(gates_hbm.at[pl.ds(0, 256)], gates.at[pl.ds(0, 256)], in_sem.at[0]),
        pltpu.make_async_copy(psi_hbm, psi_in, in_sem.at[1]),
        pltpu.make_async_copy(lam_hbm, lam_in, in_sem.at[2]),
        pltpu.make_async_copy(
            gates_hbm.at[pl.ds(256, 512)], gates.at[pl.ds(256, 512)], in_sem.at[3]
        ),
    ]
    for load in loads:
        load.start()
    lax.fori_loop(1, PLANE, greet, 0)
    for j in range(4):
        pl.semaphore_signal(barrier, inc=1, device_id=(swap_dest(j),), device_id_type=MESH)
    pl.semaphore_signal(
        barrier, inc=1, device_id=(lax.rem(y + 2, 4) * PLANE + m,), device_id_type=MESH
    )

    def build(layer):
        real_t = gates[pl.ds(layer * 256, 128), :].T
        imag_t = gates[pl.ds(layer * 256 + 128, 128), :].T
        real_high, real_low = split(real_t)
        imag_high, imag_low = split(imag_t)
        for base, real, imag in ((0, real_high, imag_high), (256, real_low, imag_low)):
            mats[layer, base:base + 128, 0:128] = real
            mats[layer, base:base + 128, 128:256] = imag
            mats[layer, base + 128:base + 256, 0:128] = -imag
            mats[layer, base + 128:base + 256, 128:256] = real

    def load_columns(read):
        for array in range(2):
            for block in range(2):
                left = (array * 2 + block) * 128
                for part in range(2):
                    high, low = split(read(array, block, part))
                    vh[part * 128:part * 128 + 128, left:left + 128] = high
                    vl[part * 128:part * 128 + 128, left:left + 128] = low

    def correlate(layer, first):
        psi_high, psi_low = vh[:, 0:256], vl[:, 0:256]
        lam_high, lam_low = vh[:, 256:512], vl[:, 256:512]
        value = (
            lax.dot_general(lam_high, psi_high, NT, preferred_element_type=F32)
            + lax.dot_general(lam_high, psi_low, NT, preferred_element_type=F32)
            + lax.dot_general(lam_low, psi_high, NT, preferred_element_type=F32)
        )
        if first:
            acc[layer] = value
        else:
            acc[layer] += value

    def apply_gate(layer):
        dims = (((1,), (0,)), ((), ()))
        return dot3(mats[layer], vh[...], vl[...], dims)

    def cut(value, array, block, part):
        left = (array * 2 + block) * 128
        return value[part * 128:part * 128 + 128, left:left + 128]

    combos = [(a, b, p) for a in range(2) for b in range(2) for p in range(2)]
    ins = (psi_in, lam_in)
    outs = (psi_res, lam_res)

    def sub(array, block, part):
        return array * 4 + block * 2 + part

    def gate0(k):
        load_columns(lambda a, b, p: ins[a][pl.ds(k * 4 + b * 2 + p, 128, stride=16), :])
        value = apply_gate(0)
        for a, b, p in combos:
            s0[k, pl.ds(sub(a, b, p), 128, stride=8), :] = cut(value, a, b, p)

    def swap_start(k):
        for j in range(4):
            remote(
                s0.at[k, pl.ds(j * 256, 256)],
                r1.at[k, pl.ds((2 * y_high + core) * 256, 256)],
                swap_send.at[k], swap_recv.at[k], swap_dest(j),
            ).start()

    def swap_wait(k):
        remote(s0.at[k], r1.at[k], swap_send.at[k], swap_recv.at[k], swap_dest(0)).wait_recv()

    def gate1(k):
        load_columns(lambda a, b, p: r1[k, pl.ds(sub(a, b, p), 128, stride=8), :])
        value = apply_gate(1)
        for a, b, p in combos:
            part = cut(value, a, b, p)
            for j in range(4):
                s1[k, pl.ds(j * 8 + sub(a, b, p), 32, stride=32), :] = part[j * 32:j * 32 + 32]

    def xz_own(k):
        return pltpu.make_async_copy(
            s1.at[k, pl.ds(m * 32, 32)], r2.at[k, pl.ds(m * 32, 32)], own_sem.at[0, k]
        )

    def xz_start(k):
        def body(i, carry):
            q = plane_peer(i)
            remote(
                s1.at[k, pl.ds(q * 32, 32)], r2.at[k, pl.ds(m * 32, 32)],
                xz_send.at[k], xz_recv.at[k], y * PLANE + q,
            ).start()
            return carry

        lax.fori_loop(1, PLANE, body, 0)
        xz_own(k).start()

    def xz_wait(k):
        remote(
            s1.at[k, pl.ds(0, 992)], r2.at[k, pl.ds(0, 992)],
            xz_send.at[k], xz_recv.at[k], swap_dest(0),
        ).wait_recv()
        xz_own(k).wait()

    r2_tiles = r2.reshape(K, 32, 4, 8, 128)
    r3_tiles = r3.reshape(K, 128, 8, 128)
    block_of_me = 2 * y_high + 1 - y_low

    def y_own(k):
        return pltpu.make_async_copy(
            r2_tiles.at[k, :, y], r3_tiles.at[k, pl.ds(block_of_me * 32, 32)], own_sem.at[1, k]
        )

    def y_start(k):
        for step in (2, 1, 3):
            to = lax.rem(y + step, 4)
            remote(
                r2_tiles.at[k, :, to], r3_tiles.at[k, pl.ds(block_of_me * 32, 32)],
                y_send.at[k], y_recv.at[k], to * PLANE + m,
            ).start()
        y_own(k).start()

    def y_wait(k):
        remote(
            r2.at[k, pl.ds(0, 768)], r3.at[k, pl.ds(0, 768)],
            y_send.at[k], y_recv.at[k], swap_dest(0),
        ).wait_recv()
        y_own(k).wait()

    def gate2_load(k):
        load_columns(lambda a, b, p: r3[k, pl.ds(sub(a, b, p), 128, stride=8), :])

    def gate2_apply(k):
        value = apply_gate(2)
        for a, b, p in combos:
            outs[a][pl.ds(k * 4 + b * 2 + p, 128, stride=16), :] = cut(value, a, b, p)

    def reduce_start(layer):
        real = acc[layer, 0:128, 0:128] + acc[layer, 128:256, 128:256]
        imag = acc[layer, 128:256, 0:128] - acc[layer, 0:128, 128:256]
        high, low = split(jnp.concatenate([real, -imag], axis=1))
        left = lax.dot_general(high, mats[layer], NT, preferred_element_type=F32)
        rest = lax.dot_general(low, mats[layer, 0:256], NT, preferred_element_type=F32)
        value = left[:, 0:256] + (left[:, 256:512] + rest)
        terms[layer, 0:128, :] = value[:, 0:128]
        terms[layer, 128:256, :] = -value[:, 128:256]
        mine = pl.ds(m * 8, 8)
        mr[layer, mine, :] = terms[layer, mine, :]

        def body(i, carry):
            q = plane_peer(i)
            remote(
                terms.at[layer, pl.ds(q * 8, 8)], mr.at[layer, mine],
                rs_send.at[layer], rs_recv.at[layer], y * PLANE + q,
            ).start()
            return carry

        lax.fori_loop(1, PLANE, body, 0)

    def reduce_middle(layer):
        remote(
            terms.at[layer, pl.ds(0, 248)], mr.at[layer, pl.ds(0, 248)],
            rs_send.at[layer], rs_recv.at[layer], swap_dest(0),
        ).wait_recv()
        total = mr[layer, 0:8, :]
        parts = [mr[layer, i * 8:i * 8 + 8, :] for i in range(PLANE)]
        while len(parts) > 1:
            parts = [parts[i] + parts[i + 1] for i in range(0, len(parts), 2)]
        total = parts[0]
        slot = pl.ds(y * 8, 8)
        yb[layer, slot, :] = total
        for step in (2, 1, 3):
            remote(
                yb.at[layer, slot], yb.at[layer, slot],
                ye_send.at[layer], ye_recv.at[layer], lax.rem(y + step, 4) * PLANE + m,
            ).start()

    def reduce_end(layer):
        remote(
            yb.at[layer, pl.ds(0, 24)], yb.at[layer, pl.ds(0, 24)],
            ye_send.at[layer], ye_recv.at[layer], swap_dest(0),
        ).wait_recv()
        total = (yb[layer, 0:8, :] + yb[layer, 8:16, :]) + (
            yb[layer, 16:24, :] + yb[layer, 24:32, :]
        )
        mine = pl.ds(m * 8, 8)
        gout[layer, mine, :] = total * scale

        def body(i, carry):
            remote(
                gout.at[layer, mine], gout.at[layer, mine],
                ag_send.at[layer], ag_recv.at[layer], y * PLANE + plane_peer(i),
            ).start()
            return carry

        lax.fori_loop(1, PLANE, body, 0)

    def reduce_wait(layer):
        remote(
            gout.at[layer, pl.ds(0, 248)], gout.at[layer, pl.ds(0, 248)],
            ag_send.at[layer], ag_recv.at[layer], swap_dest(0),
        ).wait_recv()

    loads[0].wait()
    build(0)
    loads[1].wait()
    loads[2].wait()
    for k in range(K):
        gate0(k)
        if k == 0:
            pl.semaphore_wait(barrier, PLANE - 1 + 5)
        swap_start(k)
        correlate(0, k == 0)
    loads[3].wait()
    build(1)
    reduce_start(0)
    swap_wait(0)
    gate1(0)
    xz_start(0)
    correlate(1, True)
    build(2)
    reduce_middle(0)
    swap_wait(1)
    gate1(1)
    xz_start(1)
    correlate(1, False)
    reduce_end(0)
    xz_wait(0)
    y_start(0)
    swap_wait(2)
    gate1(2)
    xz_start(2)
    correlate(1, False)
    swap_wait(3)
    gate1(3)
    xz_start(3)
    correlate(1, False)
    reduce_start(1)
    xz_wait(1)
    y_start(1)
    reduce_middle(1)
    y_wait(0)
    gate2_load(0)
    correlate(2, True)
    gate2_apply(0)
    reduce_end(1)
    xz_wait(2)
    y_start(2)
    y_wait(1)
    gate2_load(1)
    correlate(2, False)
    gate2_apply(1)
    xz_wait(3)
    y_start(3)
    y_wait(2)
    gate2_load(2)
    correlate(2, False)
    gate2_apply(2)
    y_wait(3)
    gate2_load(3)
    correlate(2, False)
    reduce_start(2)
    gate2_apply(3)
    stores = [
        pltpu.make_async_copy(psi_res, psi_out, out_sem.at[0]),
        pltpu.make_async_copy(lam_res, lam_out, out_sem.at[1]),
    ]
    for store in stores:
        store.start()
    reduce_middle(2)
    reduce_wait(0)
    reduce_wait(1)
    reduce_end(2)
    reduce_wait(2)
    grad_store = pltpu.make_async_copy(gout, grad_out, out_sem.at[2])
    grad_store.start()

    for k in range(K):
        remote(s0.at[k], r1.at[k], swap_send.at[k], swap_recv.at[k], swap_dest(0)).wait_send()
        remote(
            s1.at[k, pl.ds(0, 992)], r2.at[k, pl.ds(0, 992)],
            xz_send.at[k], xz_recv.at[k], swap_dest(0),
        ).wait_send()
        remote(
            r2.at[k, pl.ds(0, 768)], r3.at[k, pl.ds(0, 768)],
            y_send.at[k], y_recv.at[k], swap_dest(0),
        ).wait_send()
    for layer in range(3):
        remote(
            terms.at[layer, pl.ds(0, 248)], mr.at[layer, pl.ds(0, 248)],
            rs_send.at[layer], rs_recv.at[layer], swap_dest(0),
        ).wait_send()
        remote(
            yb.at[layer, pl.ds(0, 24)], yb.at[layer, pl.ds(0, 24)],
            ye_send.at[layer], ye_recv.at[layer], swap_dest(0),
        ).wait_send()
        remote(
            gout.at[layer, pl.ds(0, 248)], gout.at[layer, pl.ds(0, 248)],
            ag_send.at[layer], ag_recv.at[layer], swap_dest(0),
        ).wait_send()
    for store in stores:
        store.wait()
    grad_store.wait()


def rows_of(field):
    return field.reshape(2, 1024, 128).transpose(1, 0, 2).reshape(2048, 128)


def field_of(rows):
    return rows.reshape(1024, 2, 128).transpose(1, 0, 2).reshape(2, 131072)


def on_device(state, costate, gates):
    scale = 1.0 / math.sqrt(128 * 1024)
    dma = pltpu.SemaphoreType.DMA
    psi, lam, grads = pl.pallas_call(
        functools.partial(kernel, scale),
        out_shape=(
            jax.ShapeDtypeStruct((2048, 128), F32),
            jax.ShapeDtypeStruct((2048, 128), F32),
            jax.ShapeDtypeStruct((3, 256, 128), F32),
        ),
        in_specs=[pl.BlockSpec(memory_space=pl.ANY)] * 3,
        out_specs=[pl.BlockSpec(memory_space=pl.ANY)] * 3,
        scratch_shapes=[
            pltpu.VMEM((2048, 128), F32),
            pltpu.VMEM((2048, 128), F32),
            pltpu.VMEM((768, 128), F32),
            pltpu.VMEM((3, 512, 256), BF16),
            pltpu.VMEM((K, 1024, 128), F32),
            pltpu.VMEM((K, 1024, 128), F32),
            pltpu.VMEM((K, 1024, 128), F32),
            pltpu.VMEM((K, 1024, 128), F32),
            pltpu.VMEM((K, 1024, 128), F32),
            pltpu.VMEM((256, 512), BF16),
            pltpu.VMEM((256, 512), BF16),
            pltpu.VMEM((3, 256, 256), F32),
            pltpu.VMEM((2048, 128), F32),
            pltpu.VMEM((2048, 128), F32),
            pltpu.VMEM((3, 256, 128), F32),
            pltpu.VMEM((3, 256, 128), F32),
            pltpu.VMEM((3, 32, 128), F32),
            pltpu.VMEM((3, 256, 128), F32),
            dma((4,)), dma((3,)),
            dma((K,)), dma((K,)), dma((K,)), dma((K,)), dma((K,)), dma((K,)), dma((2, K)),
            dma((3,)), dma((3,)), dma((3,)), dma((3,)), dma((3,)), dma((3,)),
        ],
        compiler_params=pltpu.CompilerParams(collective_id=0, has_side_effects=True),
        name="window",
    )(rows_of(state), rows_of(costate), gates.reshape(768, 128))
    return field_of(psi), field_of(lam), grads.reshape(3, 2, 128, 128)


def solution(mesh):
    return jax.shard_map(
        on_device,
        mesh=mesh,
        in_specs=(P(None, "amp"), P(None, "amp"), P()),
        out_specs=(P(None, "amp"), P(None, "amp"), P()),
        check_vma=False,
    )
```

time: 439 us -> 88.4 us (0.20); the launches traced: 431 us -> 88.2 us
  waiting for transfers between devices: 193 us -> 0 us
  local copies, waits for them, and re-layouts: 123 us -> 4.33 us
  Pallas kernels: 0 us -> 83.2 us
  matrix products: 35.3 us -> 0 us
  other arithmetic: 33.1 us -> 0 us
  starting transfers between devices: 31 us -> 0 us
  between operations: 15.5 us -> 0.65 us
    psum x1 -> x0, waiting for transfers between devices: 143 us -> none  [on_device(): gradient_list.append(lax.psum(term, 'amp') * grad_scale)]
    pallas_call x0 -> x1, Pallas kernels: none -> 83.2 us  [on_device(): pl.pallas_call(functools.partial(kernel, scale), out_shape=(jax.ShapeDtyp...]
    ppermute x18 -> x0, waiting for transfers between devices: 49.9 us -> none  [swapped(): return lax.ppermute(value, axis, pairs)]
    dot_general x33 -> x0, matrix products: 35.3 us -> none  [the longest x24 22.1 us: contract(): lax.dot_general(matrix, operand, dims, precision=high, preferred_element_...]
    another operation x30 -> x0, local copies, waits for them, and re-layouts: 32.8 us -> none  [the longest x18 26 us: half_swap(): first = jnp.stack([kept_half, got_half], axis=2)]
    ppermute x18 -> x0, starting transfers between devices: 31 us -> none  [swapped(): return lax.ppermute(value, axis, pairs)]
    select_n x18 -> x0, other arithmetic: 26.3 us -> none  [half_swap(): results.append(jnp.where(own_bit == 0, first, second).reshape(shape_now))]
    unnamed x71 -> x7, local copies, waits for them, and re-layouts: 29.9 us -> 4.33 us
  transfers between devices with their start and end apart: 19 -> 0, of which waited for: 13 -> 0; matrix products, arithmetic and copies ran while one was open for 27% -> 0% of each run, Pallas kernels for 0% -> 0%
where the time goes in v1:
time: 88.4 us; the launch traced here: 88.2 us
  Pallas kernels  83.2 us (94%)
  local copies, waits for them, and re-layouts  4.33 us (5%)
    pallas_call x1, Pallas kernels, on_device(): pl.pallas_call(functools.partial(kernel, scale), out_shape=(jax.ShapeDtyp...  83.2 us
    unnamed x7, local copies, waits for them, and re-layouts  4.33 us

profile of v1, /device:TPU:1, one launch (start us, length us, event | category | flops | bytes accessed | tf_op | source)
XLA Modules:
  0.0 88.2 jit_solution(11475055706541465172)
XLA Ops:
  0.6 83.2 %window.1 = (f32[2048,128]{1,0:T(8,128)}, f32[2048,128]{1,0:T(8,128)}, f32[3,256,128]{2,1,0:T(8,128)}) custom-call(f32[2048,128]{1,0:T(8,128)} %bitcast.22, f32[2048,128]{1,0:T(8,128)} %bitcast.23, f32[768,128]{1,0:T(8,128)} %bitcast.26), custom_call_target="tpu_custom_call" | custom-call | tf_op jit(solution)/shard_map/window/pallas_call | solution.py:390
  83.9 0.0 copy-start
  83.9 2.4 %copy.13 = f32[2,131072]{1,0:T(2,128)} copy(f32[2,131072]{1,0:T(2,128)} %bitcast.25) | data formatting | bytes 2097152
  86.2 0.0 copy-done
  86.2 0.0 copy-start.1
  86.2 1.0 %copy.14 = f32[2,131072]{1,0:T(2,128)} copy(f32[2,131072]{1,0:T(2,128)S(1)} %bitcast.24) | data formatting | bytes 2097152
  87.2 0.3 copy-done.1
  87.5 0.7 copy.15
Async XLA Ops:
  83.9 2.4 %copy-start = (f32[2048,128]{1,0:T(8,128)S(1)}, f32[2048,128]{1,0:T(8,128)}, u32[]{:S(2)}) copy-start(f32[2048,128]{1,0:T(8,128)} %get-tuple-element.7) | copy-start | bytes 3145732
  86.2 1.2 %copy-start.1 = (f32[3,256,128]{2,1,0:T(8,128)S(1)}, f32[3,256,128]{2,1,0:T(8,128)}, u32[]{:S(2)}) copy-start(f32[3,256,128]{2,1,0:T(8,128)} %get-tuple-element.8) | copy-start | bytes 1179652

commit v2 on v1

--- a/solution.py
+++ b/solution.py
@@ -292,12 +292,11 @@
     xz_start(0)
     correlate(1, True)
     build(2)
-    reduce_middle(0)
     swap_wait(1)
     gate1(1)
     xz_start(1)
     correlate(1, False)
-    reduce_end(0)
+    reduce_middle(0)
     xz_wait(0)
     y_start(0)
     swap_wait(2)
@@ -311,24 +310,25 @@
     reduce_start(1)
     xz_wait(1)
     y_start(1)
-    reduce_middle(1)
     y_wait(0)
     gate2_load(0)
     correlate(2, True)
     gate2_apply(0)
-    reduce_end(1)
+    reduce_end(0)
     xz_wait(2)
     y_start(2)
+    reduce_middle(1)
+    xz_wait(3)
+    y_start(3)
     y_wait(1)
     gate2_load(1)
     correlate(2, False)
     gate2_apply(1)
-    xz_wait(3)
-    y_start(3)
     y_wait(2)
     gate2_load(2)
     correlate(2, False)
     gate2_apply(2)
+    reduce_end(1)
     y_wait(3)
     gate2_load(3)
     correlate(2, False)

time: 88.4 us -> 77.6 us (0.88)
  Pallas kernels: 83.2 us -> 72.4 us
    pallas_call x1, Pallas kernels: 83.2 us -> 72.4 us  [on_device(): pl.pallas_call(functools.partial(kernel, scale), out_shape=(jax.ShapeDtyp...]
where the time goes in v2:
time: 77.6 us; the launch traced here: 77.4 us
  Pallas kernels  72.4 us (93%)
  local copies, waits for them, and re-layouts  4.33 us (6%)
    pallas_call x1, Pallas kernels, on_device(): pl.pallas_call(functools.partial(kernel, scale), out_shape=(jax.ShapeDtyp...  72.4 us
    unnamed x7, local copies, waits for them, and re-layouts  4.33 us

profile of v2, /device:TPU:1, one launch (start us, length us, event | category | flops | bytes accessed | tf_op | source)
XLA Modules:
  0.0 77.4 jit_solution(10013746271105230690)
XLA Ops:
  0.6 72.4 %window.1 = (f32[2048,128]{1,0:T(8,128)}, f32[2048,128]{1,0:T(8,128)}, f32[3,256,128]{2,1,0:T(8,128)}) custom-call(f32[2048,128]{1,0:T(8,128)} %bitcast.22, f32[2048,128]{1,0:T(8,128)} %bitcast.23, f32[768,128]{1,0:T(8,128)} %bitcast.26), custom_call_target="tpu_custom_call" | custom-call | tf_op jit(solution)/shard_map/window/pallas_call | solution.py:390
  73.0 0.0 copy-start
  73.0 2.4 %copy.13 = f32[2,131072]{1,0:T(2,128)} copy(f32[2,131072]{1,0:T(2,128)} %bitcast.25) | data formatting | bytes 2097152
  75.4 0.0 copy-done
  75.4 0.0 copy-start.1
  75.4 1.0 %copy.14 = f32[2,131072]{1,0:T(2,128)} copy(f32[2,131072]{1,0:T(2,128)S(1)} %bitcast.24) | data formatting | bytes 2097152
  76.3 0.3 copy-done.1
  76.6 0.7 copy.15
Async XLA Ops:
  73.0 2.4 %copy-start = (f32[2048,128]{1,0:T(8,128)S(1)}, f32[2048,128]{1,0:T(8,128)}, u32[]{:S(2)}) copy-start(f32[2048,128]{1,0:T(8,128)} %get-tuple-element.7) | copy-start | bytes 3145732
  75.4 1.2 %copy-start.1 = (f32[3,256,128]{2,1,0:T(8,128)S(1)}, f32[3,256,128]{2,1,0:T(8,128)}, u32[]{:S(2)}) copy-start(f32[3,256,128]{2,1,0:T(8,128)} %get-tuple-element.8) | copy-start | bytes 1179652

commit v3 on v2

--- a/solution.py
+++ b/solution.py
@@ -29,10 +29,10 @@
 
 
 def kernel(
-    scale, psi_hbm, lam_hbm, gates_hbm, psi_out, lam_out, grad_out,
+    scale, psi_hbm, lam_hbm, gates_hbm, psi_res, lam_res, gout,
     psi_in, lam_in, gates, mats, s0, r1, s1, r2, r3, vh, vl, acc,
-    psi_res, lam_res, terms, mr, yb, gout,
-    in_sem, out_sem, swap_send, swap_recv, xz_send, xz_recv, y_send, y_recv, own_sem,
+    terms, mr, yb,
+    in_sem, entry_sem, swap_send, swap_recv, xz_send, xz_recv, y_send, y_recv, own_sem,
     rs_send, rs_recv, ye_send, ye_recv, ag_send, ag_recv,
 ):
     me = lax.axis_index("amp")
@@ -49,17 +49,35 @@
             device_id=(device,), device_id_type=MESH,
         )
 
-    def plane_peer(i):
-        return lax.rem(m + i, PLANE)
+    x, z = m // 8, lax.rem(m // 2, 4)
+
+    def peer(dx, dz, other):
+        return lax.rem(x + dx, 4) * 8 + lax.rem(z + dz, 4) * 2 + lax.rem(core + other, 2)
+
+    def at(dy, dx, dz, other):
+        return lax.rem(y + dy, 4) * PLANE + peer(dx, dz, other)
+
+    hops = (0, 1, 2, 1)
+    offsets = [(dx, dz, o) for dx in range(4) for dz in range(4) for o in range(2)]
+    offsets = sorted(offsets, key=lambda d: -(hops[d[0]] + hops[d[1]]))[:-2] + [(0, 0, 1)]
 
     def swap_dest(j):
         return (2 * (j // 2) + 1 - y_low) * PLANE + (m - core) + j % 2
 
-    def greet(i, carry):
-        pl.semaphore_signal(
-            barrier, inc=1, device_id=(y * PLANE + plane_peer(i),), device_id_type=MESH
-        )
-        return carry
+    near = [(dy, 0, 0, o) for dy in (1, 3) for o in range(2)]
+    near += [(0, dx, 0, o) for dx in (1, 3) for o in range(2)]
+    near += [(0, 0, dz, o) for dz in (1, 3) for o in range(2)] + [(0, 0, 0, 1)]
+    rounds = (
+        [(dy, 0, 0, 0) for dy in (1, 3)] + [(0, dx, 0, 0) for dx in (1, 3)],
+        [(0, 0, dz, 0) for dz in (1, 3)],
+        [(0, 0, dz, 0) for dz in (1, 3)],
+    )
+
+    def tell(semaphore, where):
+        for offset in where:
+            pl.semaphore_signal(
+                semaphore, inc=1, device_id=(at(*offset),), device_id_type=MESH
+            )
 
     loads = [
         pltpu.make_async_copy(gates_hbm.at[pl.ds(0, 256)], gates.at[pl.ds(0, 256)], in_sem.at[0]),
@@ -71,12 +89,7 @@
     ]
     for load in loads:
         load.start()
-    lax.fori_loop(1, PLANE, greet, 0)
-    for j in range(4):
-        pl.semaphore_signal(barrier, inc=1, device_id=(swap_dest(j),), device_id_type=MESH)
-    pl.semaphore_signal(
-        barrier, inc=1, device_id=(lax.rem(y + 2, 4) * PLANE + m,), device_id_type=MESH
-    )
+    tell(barrier, near)
 
     def build(layer):
         real_t = gates[pl.ds(layer * 256, 128), :].T
@@ -157,15 +170,12 @@
         )
 
     def xz_start(k):
-        def body(i, carry):
-            q = plane_peer(i)
+        for offset in offsets:
+            q = peer(*offset)
             remote(
                 s1.at[k, pl.ds(q * 32, 32)], r2.at[k, pl.ds(m * 32, 32)],
                 xz_send.at[k], xz_recv.at[k], y * PLANE + q,
             ).start()
-            return carry
-
-        lax.fori_loop(1, PLANE, body, 0)
         xz_own(k).start()
 
     def xz_wait(k):
@@ -220,15 +230,12 @@
         mine = pl.ds(m * 8, 8)
         mr[layer, mine, :] = terms[layer, mine, :]
 
-        def body(i, carry):
-            q = plane_peer(i)
+        for offset in offsets:
+            q = peer(*offset)
             remote(
                 terms.at[layer, pl.ds(q * 8, 8)], mr.at[layer, mine],
                 rs_send.at[layer], rs_recv.at[layer], y * PLANE + q,
             ).start()
-            return carry
-
-        lax.fori_loop(1, PLANE, body, 0)
 
     def reduce_middle(layer):
         remote(
@@ -259,14 +266,11 @@
         mine = pl.ds(m * 8, 8)
         gout[layer, mine, :] = total * scale
 
-        def body(i, carry):
+        for offset in offsets:
             remote(
                 gout.at[layer, mine], gout.at[layer, mine],
-                ag_send.at[layer], ag_recv.at[layer], y * PLANE + plane_peer(i),
-            ).start()
-            return carry
-
-        lax.fori_loop(1, PLANE, body, 0)
+                ag_send.at[layer], ag_recv.at[layer], y * PLANE + peer(*offset),
+            ).start()
 
     def reduce_wait(layer):
         remote(
@@ -281,7 +285,11 @@
     for k in range(K):
         gate0(k)
         if k == 0:
-            pl.semaphore_wait(barrier, PLANE - 1 + 5)
+            pl.semaphore_wait(barrier, len(near))
+        else:
+            pl.semaphore_wait(entry_sem.at[k - 1], len(rounds[k - 1]))
+        if k < 3:
+            tell(entry_sem.at[k], rounds[k])
         swap_start(k)
         correlate(0, k == 0)
     loads[3].wait()
@@ -334,19 +342,11 @@
     correlate(2, False)
     reduce_start(2)
     gate2_apply(3)
-    stores = [
-        pltpu.make_async_copy(psi_res, psi_out, out_sem.at[0]),
-        pltpu.make_async_copy(lam_res, lam_out, out_sem.at[1]),
-    ]
-    for store in stores:
-        store.start()
     reduce_middle(2)
     reduce_wait(0)
     reduce_wait(1)
     reduce_end(2)
     reduce_wait(2)
-    grad_store = pltpu.make_async_copy(gout, grad_out, out_sem.at[2])
-    grad_store.start()
 
     for k in range(K):
         remote(s0.at[k], r1.at[k], swap_send.at[k], swap_recv.at[k], swap_dest(0)).wait_send()
@@ -371,9 +371,17 @@
             gout.at[layer, pl.ds(0, 248)], gout.at[layer, pl.ds(0, 248)],
             ag_send.at[layer], ag_recv.at[layer], swap_dest(0),
         ).wait_send()
-    for store in stores:
-        store.wait()
-    grad_store.wait()
+
+
+def store_kernel(psi_res, lam_res, gout, psi_out, lam_out, grad_out, sem):
+    copies = [
+        pltpu.make_async_copy(src, dst, sem.at[i])
+        for i, (src, dst) in enumerate(((psi_res, psi_out), (lam_res, lam_out), (gout, grad_out)))
+    ]
+    for copy in copies:
+        copy.start()
+    for copy in copies:
+        copy.wait()
 
 
 def rows_of(field):
@@ -387,15 +395,12 @@
 def on_device(state, costate, gates):
     scale = 1.0 / math.sqrt(128 * 1024)
     dma = pltpu.SemaphoreType.DMA
-    psi, lam, grads = pl.pallas_call(
+    shapes = ((2048, 128), (2048, 128), (3, 256, 128))
+    results = pl.pallas_call(
         functools.partial(kernel, scale),
-        out_shape=(
-            jax.ShapeDtypeStruct((2048, 128), F32),
-            jax.ShapeDtypeStruct((2048, 128), F32),
-            jax.ShapeDtypeStruct((3, 256, 128), F32),
-        ),
+        out_shape=tuple(pltpu.VMEM(shape, F32) for shape in shapes),
         in_specs=[pl.BlockSpec(memory_space=pl.ANY)] * 3,
-        out_specs=[pl.BlockSpec(memory_space=pl.ANY)] * 3,
+        out_specs=[pl.BlockSpec(memory_space=pltpu.VMEM)] * 3,
         scratch_shapes=[
             pltpu.VMEM((2048, 128), F32),
             pltpu.VMEM((2048, 128), F32),
@@ -409,19 +414,24 @@
             pltpu.VMEM((256, 512), BF16),
             pltpu.VMEM((256, 512), BF16),
             pltpu.VMEM((3, 256, 256), F32),
-            pltpu.VMEM((2048, 128), F32),
-            pltpu.VMEM((2048, 128), F32),
             pltpu.VMEM((3, 256, 128), F32),
             pltpu.VMEM((3, 256, 128), F32),
             pltpu.VMEM((3, 32, 128), F32),
-            pltpu.VMEM((3, 256, 128), F32),
-            dma((4,)), dma((3,)),
+            dma((4,)), pltpu.SemaphoreType.REGULAR((3,)),
             dma((K,)), dma((K,)), dma((K,)), dma((K,)), dma((K,)), dma((K,)), dma((2, K)),
             dma((3,)), dma((3,)), dma((3,)), dma((3,)), dma((3,)), dma((3,)),
         ],
         compiler_params=pltpu.CompilerParams(collective_id=0, has_side_effects=True),
         name="window",
     )(rows_of(state), rows_of(costate), gates.reshape(768, 128))
+    psi, lam, grads = pl.pallas_call(
+        store_kernel,
+        out_shape=tuple(jax.ShapeDtypeStruct(shape, F32) for shape in shapes),
+        in_specs=[pl.BlockSpec(memory_space=pltpu.VMEM)] * 3,
+        out_specs=[pl.BlockSpec(memory_space=pl.ANY)] * 3,
+        scratch_shapes=[dma((3,))],
+        name="store",
+    )(*(pltpu.with_memory_space_constraint(r, pltpu.VMEM) for r in results))
     return field_of(psi), field_of(lam), grads.reshape(3, 2, 128, 128)
 
 

time: 77.6 us -> 71.4 us (0.920)
  local copies, waits for them, and re-layouts: 4.33 us -> 0 us
  Pallas kernels: 72.4 us -> 70.6 us
    unnamed x7 -> x0, local copies, waits for them, and re-layouts: 4.33 us -> none
    pallas_call x1 -> x2, Pallas kernels: 72.4 us -> 70.6 us  [the longest x1 69.2 us: on_device(): pl.pallas_call(functools.partial(kernel, scale), out_shape=tuple((pltpu.V...]
where the time goes in v3:
time: 71.4 us; the launch traced here: 71.3 us
  Pallas kernels  70.6 us (99%)
    pallas_call x1, Pallas kernels, on_device(): pl.pallas_call(functools.partial(kernel, scale), out_shape=tuple((pltpu.V...  69.2 us
    pallas_call x1, Pallas kernels, on_device(): pl.pallas_call(store_kernel, out_shape=tuple((jax.ShapeDtypeStruct(shape,...  1.46 us

profile of v3, /device:TPU:1, one launch (start us, length us, event | category | flops | bytes accessed | tf_op | source)
XLA Modules:
  0.0 71.3 jit_solution(15233184481105146030)
XLA Ops:
  0.6 69.2 %window.1 = (f32[2048,128]{1,0:T(8,128)S(1)}, f32[2048,128]{1,0:T(8,128)S(1)}, f32[3,256,128]{2,1,0:T(8,128)S(1)}) custom-call(f32[2048,128]{1,0:T(8,128)} %bitcast.22, f32[2048,128]{1,0:T(8,128)} %bitcast.23, f32[768,128]{1,0:T(8,128)} %bitcast.24), custom_call_target="tpu_custom_call" | custom-call | tf_op jit(solution)/shard_map/window/pallas_call | solution.py:399
  69.8 1.5 %store.1 = (f32[2048,128]{1,0:T(8,128)}, f32[2048,128]{1,0:T(8,128)}, f32[3,256,128]{2,1,0:T(8,128)}) custom-call(f32[2048,128]{1,0:T(8,128)S(1)} %get-tuple-element.9.psi_res, f32[2048,128]{1,0:T(8,128)S(1)} %get-tuple-element.10.lam_res, f32[3,256,128]{2,1,0:T(8,128)S(1)} %get-tuple-element.11.gout), custom_call_target="tpu_custom_call" | custom-call | tf_op jit(solution)/shard_map/store/pallas_call | solution.py:427

commit v4 on v3

v4 whole, which is shorter than its diff:
```python
import functools
import math

import jax
import jax.numpy as jnp
from jax import lax
from jax.experimental import pallas as pl
from jax.experimental.pallas import tpu as pltpu
from jax.sharding import PartitionSpec as P

F32 = jnp.float32
BF16 = jnp.bfloat16
MESH = pl.DeviceIdType.MESH
K = 4
PLANE = 32
NN = (((1,), (0,)), ((), ()))
NT = (((1,), (1,)), ((), ()))
TN = (((0,), (0,)), ((), ()))


def split(value):
    high = value.astype(BF16)
    return high, (value - high.astype(F32)).astype(BF16)


def dot3(stacked, high, low, dims):
    rows = stacked.shape[0] // 2
    both = lax.dot_general(stacked, high, dims, preferred_element_type=F32)
    rest = lax.dot_general(stacked[:rows], low, dims, preferred_element_type=F32)
    return both[:rows] + (both[rows:] + rest)


def kernel(
    scale, psi_hbm, lam_hbm, gates_hbm, psi_res, lam_res, gout,
    psi_in, lam_in, gates, mats, s1, r1, f1, s2, r2, f2, xb, zb, vh, vl, wh, wl, acc,
    terms, cb, hb, mr, yb,
    in_sem, entry_sem, st_send, st_recv, own_sem, red_send, red_recv,
):
    me = lax.axis_index("amp")
    y = me // PLANE
    m = lax.rem(me, PLANE)
    core = lax.rem(me, 2)
    x, z = m // 8, lax.rem(m // 2, 4)
    chip = m // 2
    barrier = pltpu.get_barrier_semaphore()

    def remote(src, dst, send, recv, device):
        return pltpu.make_async_remote_copy(
            src_ref=src, dst_ref=dst, send_sem=send, recv_sem=recv,
            device_id=(device,), device_id_type=MESH,
        )

    def peer(dx, dz, other):
        return lax.rem(x + dx, 4) * 8 + lax.rem(z + dz, 4) * 2 + lax.rem(core + other, 2)

    def at(dy, dx, dz, other):
        return lax.rem(y + dy, 4) * PLANE + peer(dx, dz, other)

    hops = (0, 1, 2, 1)
    offsets = [(dx, dz, o) for dx in range(4) for dz in range(4) for o in range(2)]
    offsets = sorted(offsets, key=lambda d: -(hops[d[0]] + hops[d[1]]))[:-2] + [(0, 0, 1)]
    same_core = [d for d in offsets if d[2] == 0]
    partner = at(0, 0, 0, 1)

    near = [(dy, 0, 0, 0) for dy in (2, 1, 3)]
    near += [(0, dx, 0, o) for dx in (1, 3) for o in range(2)]
    near += [(0, 0, dz, o) for dz in (1, 3) for o in range(2)] + [(0, 0, 0, 1)]
    rounds = (
        [(0, dx, 0, 0) for dx in (1, 3)],
        [(0, 0, dz, 0) for dz in (1, 3)],
        [(0, 0, dz, 0) for dz in (1, 3)],
    )

    def tell(semaphore, where):
        for offset in where:
            pl.semaphore_signal(
                semaphore, inc=1, device_id=(at(*offset),), device_id_type=MESH
            )

    def hear(i):
        pl.semaphore_wait(entry_sem.at[i], len(rounds[i]))

    loads = [
        pltpu.make_async_copy(gates_hbm.at[pl.ds(0, 256)], gates.at[pl.ds(0, 256)], in_sem.at[0]),
        pltpu.make_async_copy(psi_hbm, psi_in, in_sem.at[1]),
        pltpu.make_async_copy(lam_hbm, lam_in, in_sem.at[2]),
        pltpu.make_async_copy(
            gates_hbm.at[pl.ds(256, 512)], gates.at[pl.ds(256, 512)], in_sem.at[3]
        ),
    ]
    for load in loads:
        load.start()
    tell(barrier, near)

    def build(layer):
        real_t = gates[pl.ds(layer * 256, 128), :].T
        imag_t = gates[pl.ds(layer * 256 + 128, 128), :].T
        real_high, real_low = split(real_t)
        imag_high, imag_low = split(imag_t)
        for base, real, imag in ((0, real_high, imag_high), (256, real_low, imag_low)):
            mats[layer, base:base + 128, 0:128] = real
            mats[layer, base:base + 128, 128:256] = imag
            mats[layer, base + 128:base + 256, 0:128] = -imag
            mats[layer, base + 128:base + 256, 128:256] = real

    combos = [(a, b, p) for a in range(2) for b in range(2) for p in range(2)]
    ins = (psi_in, lam_in)
    outs = (psi_res, lam_res)

    def sub(array, block, part):
        return array * 4 + block * 2 + part

    def correlate(layer, first, lam, psi, dims):
        lam_high, lam_low = lam
        psi_high, psi_low = psi
        value = (
            lax.dot_general(lam_high, psi_high, dims, preferred_element_type=F32)
            + lax.dot_general(lam_high, psi_low, dims, preferred_element_type=F32)
            + lax.dot_general(lam_low, psi_high, dims, preferred_element_type=F32)
        )
        if first:
            acc[layer] = value
        else:
            acc[layer] += value

    def gate0(k, first):
        for a, b, p in combos:
            left = (a * 2 + b) * 128
            high, low = split(ins[a][pl.ds(k * 4 + b * 2 + p, 128, stride=16), :])
            vh[p * 128:p * 128 + 128, left:left + 128] = high
            vl[p * 128:p * 128 + 128, left:left + 128] = low
        value = dot3(mats[0], vh[...], vl[...], NN)
        for a, b, p in combos:
            left = (a * 2 + b) * 128
            part = value[p * 128:p * 128 + 128, left:left + 128]
            s1[k, pl.ds(sub(a, b, p), 128, stride=8), :] = part.T

    def grad0(k, first):
        correlate(
            0, first, (vh[:, 256:512], vl[:, 256:512]), (vh[:, 0:256], vl[:, 0:256]), NT
        )

    def load_rows(ref):
        for a, b, p in combos:
            top = (a * 2 + b) * 128
            high, low = split(ref[pl.ds(sub(a, b, p), 128, stride=8), :])
            wh[top:top + 128, p * 128:p * 128 + 128] = high
            wl[top:top + 128, p * 128:p * 128 + 128] = low

    def grad_rows(layer, first):
        correlate(layer, first, (wh[256:512], wl[256:512]), (wh[0:256], wl[0:256]), TN)

    f1_bits = f1.reshape(K, 2, 32, 2, 8, 128)
    xb_bits = xb.reshape(2, 32, 2, 8, 128)
    group = lax.broadcasted_iota(jnp.int32, (256, 128), 1) // 32

    def middle(k, first):
        parts = [f1_bits[k, i // 2, :, i % 2].reshape(256, 128) for i in range(4)]
        for j in range(4):
            turned = [
                parts[i] if i == j else pltpu.roll(parts[i], ((i - j) % 4) * 32, 1)
                for i in range(4)
            ]
            low_half = jnp.where(group == 0, turned[0], turned[1])
            high_half = jnp.where(group == 2, turned[2], turned[3])
            value = jnp.where(group < 2, low_half, high_half)
            xb_bits[j // 2, :, j % 2] = value.reshape(32, 8, 128)
        load_rows(xb)
        value = dot3(mats[1], wh[...], wl[...], NT)
        for a, b, p in combos:
            left = (a * 2 + b) * 128
            zb[pl.ds(sub(a, b, p), 128, stride=8), :] = (
                value[p * 128:p * 128 + 128, left:left + 128]
            )
        grad_rows(1, first)
        load_rows(zb)
        both = lax.dot_general(wh[...], mats[2], NT, preferred_element_type=F32)
        rest = lax.dot_general(wl[...], mats[2, 0:256], NT, preferred_element_type=F32)
        value = both[:, 0:256] + (both[:, 256:512] + rest)
        for a, b, p in combos:
            top = (a * 2 + b) * 128
            s2[k, pl.ds(sub(a, b, p), 128, stride=8), :] = (
                value[top:top + 128, p * 128:p * 128 + 128]
            )

    def finish(k):
        for a, b, p in combos:
            outs[a][pl.ds(k * 4 + b * 2 + p, 128, stride=16), :] = (
                f2[k, pl.ds(sub(a, b, p), 128, stride=8), :].T
            )

    def tiles(ref):
        return ref.reshape(K, 4, PLANE, 8, 128)

    def plane_start(st, src, dst, k):
        src_t, dst_t = tiles(src), tiles(dst)
        for offset in offsets:
            q = peer(*offset)
            remote(
                src_t.at[k, :, q], dst_t.at[k, :, m],
                st_send.at[st, k], st_recv.at[st, k], y * PLANE + q,
            ).start()
        pltpu.make_async_copy(src_t.at[k, :, m], dst_t.at[k, :, m], own_sem.at[st, k]).start()

    def plane_wait(st, src, dst, k, arrived=True):
        whole = remote(
            src.at[k, pl.ds(0, 992)], dst.at[k, pl.ds(0, 992)],
            st_send.at[st, k], st_recv.at[st, k], partner,
        )
        if not arrived:
            whole.wait_send()
            return
        whole.wait_recv()
        src_t, dst_t = tiles(src), tiles(dst)
        pltpu.make_async_copy(src_t.at[k, :, m], dst_t.at[k, :, m], own_sem.at[st, k]).wait()

    def y_start(st, src, dst, k):
        src_t, dst_t = tiles(src), tiles(dst)
        for step in (2, 1, 3):
            to = lax.rem(y + step, 4)
            remote(
                src_t.at[k, to], dst_t.at[k, y],
                st_send.at[st, k], st_recv.at[st, k], to * PLANE + m,
            ).start()
        pltpu.make_async_copy(src_t.at[k, y], dst_t.at[k, y], own_sem.at[st, k]).start()

    def y_wait(st, src, dst, k, arrived=True):
        whole = remote(
            src.at[k, pl.ds(0, 768)], dst.at[k, pl.ds(0, 768)],
            st_send.at[st, k], st_recv.at[st, k], partner,
        )
        if not arrived:
            whole.wait_send()
            return
        whole.wait_recv()
        src_t, dst_t = tiles(src), tiles(dst)
        pltpu.make_async_copy(src_t.at[k, y], dst_t.at[k, y], own_sem.at[st, k]).wait()

    buffers = ((s1, r1), (r1, f1), (s2, r2), (r2, f2))
    y_stage = [[k % 2 == (0 if st in (0, 3) else 1) for k in range(K)] for st in range(4)]

    def go(st, k):
        (y_start if y_stage[st][k] else plane_start)(st, *buffers[st], k)

    def got(st, k, arrived=True):
        (y_wait if y_stage[st][k] else plane_wait)(st, *buffers[st], k, arrived)

    def red(step, layer, src, dst, device):
        return remote(
            src, dst, red_send.at[step, layer], red_recv.at[step, layer], device
        )

    mine = pl.ds((core * 16 + chip) * 8, 8)
    slot = pl.ds(chip * 8, 8)
    y_slot = pl.ds(y * 8, 8)
    own_half = pl.ds(core * 128, 128)
    other_half = pl.ds((1 - core) * 128, 128)

    def pair_copy(layer):
        return red(0, layer, terms.at[layer, other_half], cb.at[layer], partner)

    def back_copy(layer):
        return red(4, layer, gout.at[layer, own_half], gout.at[layer, own_half], partner)

    def all_of(step, layer):
        if step == 0:
            return pair_copy(layer)
        if step == 1:
            part = pl.ds(0, 120)
            return red(1, layer, hb.at[layer, part], mr.at[layer, part], partner)
        if step == 2:
            part = pl.ds(0, 24)
            return red(2, layer, yb.at[layer, part], yb.at[layer, part], partner)
        if step == 3:
            part = pl.ds(0, 120)
            return red(3, layer, gout.at[layer, part], gout.at[layer, part], partner)
        return back_copy(layer)

    def reduce0(layer):
        real = acc[layer, 0:128, 0:128] + acc[layer, 128:256, 128:256]
        imag = acc[layer, 128:256, 0:128] - acc[layer, 0:128, 128:256]
        high, low = split(jnp.concatenate([real, -imag], axis=1))
        left = lax.dot_general(high, mats[layer], NT, preferred_element_type=F32)
        rest = lax.dot_general(low, mats[layer, 0:256], NT, preferred_element_type=F32)
        value = left[:, 0:256] + (left[:, 256:512] + rest)
        terms[layer, 0:128, :] = value[:, 0:128]
        terms[layer, 128:256, :] = -value[:, 128:256]
        pair_copy(layer).start()

    def reduce1(layer):
        all_of(0, layer).wait_recv()
        hb[layer] = terms[layer, own_half, :] + cb[layer]
        mr[layer, slot, :] = hb[layer, slot, :]
        for offset in same_core:
            q = peer(*offset)
            red(
                1, layer, hb.at[layer, pl.ds((q // 2) * 8, 8)], mr.at[layer, slot],
                y * PLANE + q,
            ).start()

    def reduce2(layer):
        all_of(1, layer).wait_recv()
        parts = [mr[layer, i * 8:i * 8 + 8, :] for i in range(16)]
        while len(parts) > 1:
            parts = [parts[i] + parts[i + 1] for i in range(0, len(parts), 2)]
        yb[layer, y_slot, :] = parts[0]
        for step in (2, 1, 3):
            red(
                2, layer, yb.at[layer, y_slot], yb.at[layer, y_slot],
                lax.rem(y + step, 4) * PLANE + m,
            ).start()

    def reduce3(layer):
        all_of(2, layer).wait_recv()
        total = (yb[layer, 0:8, :] + yb[layer, 8:16, :]) + (
            yb[layer, 16:24, :] + yb[layer, 24:32, :]
        )
        gout[layer, mine, :] = total * scale
        for offset in same_core:
            red(
                3, layer, gout.at[layer, mine], gout.at[layer, mine],
                y * PLANE + peer(*offset),
            ).start()

    def reduce4(layer):
        all_of(3, layer).wait_recv()
        back_copy(layer).start()

    def reduce5(layer):
        all_of(4, layer).wait_recv()

    loads[0].wait()
    build(0)
    loads[1].wait()
    loads[2].wait()
    gate0(0, True)
    pl.semaphore_wait(barrier, len(near))
    tell(entry_sem.at[0], rounds[0])
    go(0, 0)
    grad0(0, True)
    gate0(1, False)
    hear(0)
    tell(entry_sem.at[1], rounds[1])
    grad0(1, False)
    hear(1)
    tell(entry_sem.at[2], rounds[2])
    hear(2)
    go(0, 1)
    gate0(2, False)
    go(0, 2)
    grad0(2, False)
    gate0(3, False)
    go(0, 3)
    grad0(3, False)
    loads[3].wait()
    build(1)
    build(2)
    reduce0(0)
    got(0, 0)
    go(1, 0)
    reduce1(0)
    got(0, 1)
    go(1, 1)
    got(0, 2)
    go(1, 2)
    got(0, 3)
    go(1, 3)
    got(1, 1)
    middle(1, True)
    go(2, 1)
    grad_rows(2, True)
    got(1, 0)
    middle(0, False)
    go(2, 0)
    grad_rows(2, False)
    reduce2(0)
    got(1, 3)
    middle(3, False)
    go(2, 3)
    grad_rows(2, False)
    got(1, 2)
    middle(2, False)
    grad_rows(2, False)
    reduce0(2)
    reduce0(1)
    reduce1(2)
    reduce1(1)
    go(2, 2)
    got(2, 1)
    go(3, 1)
    reduce3(0)
    got(2, 0)
    reduce2(2)
    reduce2(1)
    go(3, 0)
    got(2, 3)
    reduce3(2)
    reduce3(1)
    go(3, 3)
    got(2, 2)
    go(3, 2)
    reduce4(0)
    got(3, 1)
    finish(1)
    got(3, 0)
    finish(0)
    reduce4(2)
    reduce4(1)
    got(3, 2)
    finish(2)
    got(3, 3)
    finish(3)
    for layer in range(3):
        reduce5(layer)

    for st in range(4):
        for k in range(K):
            got(st, k, False)
    for step in range(5):
        for layer in range(3):
            all_of(step, layer).wait_send()


def store_kernel(psi_res, lam_res, gout, psi_out, lam_out, grad_out, sem):
    copies = [
        pltpu.make_async_copy(src, dst, sem.at[i])
        for i, (src, dst) in enumerate(((psi_res, psi_out), (lam_res, lam_out), (gout, grad_out)))
    ]
    for copy in copies:
        copy.start()
    for copy in copies:
        copy.wait()


def rows_of(field):
    return field.reshape(2, 1024, 128).transpose(1, 0, 2).reshape(2048, 128)


def field_of(rows):
    return rows.reshape(1024, 2, 128).transpose(1, 0, 2).reshape(2, 131072)


def on_device(state, costate, gates):
    scale = 1.0 / math.sqrt(128 * 1024)
    dma = pltpu.SemaphoreType.DMA
    shapes = ((2048, 128), (2048, 128), (3, 256, 128))
    results = pl.pallas_call(
        functools.partial(kernel, scale),
        out_shape=tuple(pltpu.VMEM(shape, F32) for shape in shapes),
        in_specs=[pl.BlockSpec(memory_space=pl.ANY)] * 3,
        out_specs=[pl.BlockSpec(memory_space=pltpu.VMEM)] * 3,
        scratch_shapes=[
            pltpu.VMEM((2048, 128), F32),
            pltpu.VMEM((2048, 128), F32),
            pltpu.VMEM((768, 128), F32),
            pltpu.VMEM((3, 512, 256), BF16),
        ]
        + [pltpu.VMEM((K, 1024, 128), F32)] * 6
        + [
            pltpu.VMEM((1024, 128), F32),
            pltpu.VMEM((1024, 128), F32),
            pltpu.VMEM((256, 512), BF16),
            pltpu.VMEM((256, 512), BF16),
            pltpu.VMEM((512, 256), BF16),
            pltpu.VMEM((512, 256), BF16),
            pltpu.VMEM((3, 256, 256), F32),
            pltpu.VMEM((3, 256, 128), F32),
            pltpu.VMEM((3, 128, 128), F32),
            pltpu.VMEM((3, 128, 128), F32),
            pltpu.VMEM((3, 128, 128), F32),
            pltpu.VMEM((3, 32, 128), F32),
            dma((4,)), pltpu.SemaphoreType.REGULAR((3,)),
            dma((4, K)), dma((4, K)), dma((4, K)), dma((5, 3)), dma((5, 3)),
        ],
        compiler_params=pltpu.CompilerParams(collective_id=0, has_side_effects=True),
        name="window",
    )(rows_of(state), rows_of(costate), gates.reshape(768, 128))
    psi, lam, grads = pl.pallas_call(
        store_kernel,
        out_shape=tuple(jax.ShapeDtypeStruct(shape, F32) for shape in shapes),
        in_specs=[pl.BlockSpec(memory_space=pltpu.VMEM)] * 3,
        out_specs=[pl.BlockSpec(memory_space=pl.ANY)] * 3,
        scratch_shapes=[dma((3,))],
        name="store",
    )(*(pltpu.with_memory_space_constraint(r, pltpu.VMEM) for r in results))
    return field_of(psi), field_of(lam), grads.reshape(3, 2, 128, 128)


def solution(mesh):
    return jax.shard_map(
        on_device,
        mesh=mesh,
        in_specs=(P(None, "amp"), P(None, "amp"), P()),
        out_specs=(P(None, "amp"), P(None, "amp"), P()),
        check_vma=False,
    )
```

time: 71.4 us -> 68.9 us (0.965)
  Pallas kernels: 70.6 us -> 68.1 us
    pallas_call x1, Pallas kernels: 69.2 us -> 66.7 us  [on_device(): pl.pallas_call(functools.partial(kernel, scale), out_shape=tuple((pltpu.V...]
where the time goes in v4:
time: 68.9 us; the launch traced here: 68.8 us
  Pallas kernels  68.1 us (99%)
    pallas_call x1, Pallas kernels, on_device(): pl.pallas_call(functools.partial(kernel, scale), out_shape=tuple((pltpu.V...  66.7 us
    pallas_call x1, Pallas kernels, on_device(): pl.pallas_call(store_kernel, out_shape=tuple((jax.ShapeDtypeStruct(shape,...  1.46 us

profile of v4, /device:TPU:1, one launch (start us, length us, event | category | flops | bytes accessed | tf_op | source)
XLA Modules:
  0.0 68.8 jit_solution(6541513424358202357)
XLA Ops:
  0.6 66.7 %window.1 = (f32[2048,128]{1,0:T(8,128)S(1)}, f32[2048,128]{1,0:T(8,128)S(1)}, f32[3,256,128]{2,1,0:T(8,128)S(1)}) custom-call(f32[2048,128]{1,0:T(8,128)} %bitcast.22, f32[2048,128]{1,0:T(8,128)} %bitcast.23, f32[768,128]{1,0:T(8,128)} %bitcast.24), custom_call_target="tpu_custom_call" | custom-call | tf_op jit(solution)/shard_map/window/pallas_call | solution.py:447
  67.3 1.5 %store.1 = (f32[2048,128]{1,0:T(8,128)}, f32[2048,128]{1,0:T(8,128)}, f32[3,256,128]{2,1,0:T(8,128)}) custom-call(f32[2048,128]{1,0:T(8,128)S(1)} %get-tuple-element.9.psi_res, f32[2048,128]{1,0:T(8,128)S(1)} %get-tuple-element.10.lam_res, f32[3,256,128]{2,1,0:T(8,128)S(1)} %get-tuple-element.11.gout), custom_call_target="tpu_custom_call" | custom-call | tf_op jit(solution)/shard_map/store/pallas_call | solution.py:478

commit v5 on v4

--- a/solution.py
+++ b/solution.py
@@ -66,10 +66,14 @@
     near += [(0, dx, 0, o) for dx in (1, 3) for o in range(2)]
     near += [(0, 0, dz, o) for dz in (1, 3) for o in range(2)] + [(0, 0, 0, 1)]
     rounds = (
-        [(0, dx, 0, 0) for dx in (1, 3)],
-        [(0, 0, dz, 0) for dz in (1, 3)],
-        [(0, 0, dz, 0) for dz in (1, 3)],
+        [(0, dx, 0, 0) for dx in (1, 3)] + [(0, 0, dz, 0) for dz in (1, 3)],
+        [(0, 2, 0, 0), (0, 0, 2, 0)],
     )
+
+    def reach(d):
+        return hops[d[0]] + hops[d[1]]
+
+    known = [[d for d in offsets if reach(d) in span] for span in ((0, 1), (2,), (3, 4))]
 
     def tell(semaphore, where):
         for offset in where:
@@ -192,15 +196,17 @@
     def tiles(ref):
         return ref.reshape(K, 4, PLANE, 8, 128)
 
-    def plane_start(st, src, dst, k):
+    def plane_start(st, src, dst, k, where=offsets):
         src_t, dst_t = tiles(src), tiles(dst)
-        for offset in offsets:
+        for offset in where:
             q = peer(*offset)
             remote(
                 src_t.at[k, :, q], dst_t.at[k, :, m],
                 st_send.at[st, k], st_recv.at[st, k], y * PLANE + q,
             ).start()
-        pltpu.make_async_copy(src_t.at[k, :, m], dst_t.at[k, :, m], own_sem.at[st, k]).start()
+        if where[-1] == (0, 0, 1):
+            own = pltpu.make_async_copy(src_t.at[k, :, m], dst_t.at[k, :, m], own_sem.at[st, k])
+            own.start()
 
     def plane_wait(st, src, dst, k, arrived=True):
         whole = remote(
@@ -333,21 +339,21 @@
     build(0)
     loads[1].wait()
     loads[2].wait()
-    gate0(0, True)
+    gate0(1, True)
     pl.semaphore_wait(barrier, len(near))
     tell(entry_sem.at[0], rounds[0])
+    plane_start(0, s1, r1, 1, known[0])
+    grad0(1, True)
+    gate0(0, False)
     go(0, 0)
-    grad0(0, True)
-    gate0(1, False)
     hear(0)
     tell(entry_sem.at[1], rounds[1])
-    grad0(1, False)
-    hear(1)
-    tell(entry_sem.at[2], rounds[2])
-    hear(2)
-    go(0, 1)
+    plane_start(0, s1, r1, 1, known[1])
+    grad0(0, False)
     gate0(2, False)
     go(0, 2)
+    hear(1)
+    plane_start(0, s1, r1, 1, known[2])
     grad0(2, False)
     gate0(3, False)
     go(0, 3)
@@ -380,25 +386,25 @@
     grad_rows(2, False)
     got(1, 2)
     middle(2, False)
+    go(2, 2)
     grad_rows(2, False)
     reduce0(2)
     reduce0(1)
     reduce1(2)
     reduce1(1)
-    go(2, 2)
     got(2, 1)
     go(3, 1)
     reduce3(0)
     got(2, 0)
+    go(3, 0)
     reduce2(2)
     reduce2(1)
-    go(3, 0)
     got(2, 3)
-    reduce3(2)
-    reduce3(1)
     go(3, 3)
     got(2, 2)
     go(3, 2)
+    reduce3(2)
+    reduce3(1)
     reduce4(0)
     got(3, 1)
     finish(1)
@@ -469,7 +475,7 @@
             pltpu.VMEM((3, 128, 128), F32),
             pltpu.VMEM((3, 128, 128), F32),
             pltpu.VMEM((3, 32, 128), F32),
-            dma((4,)), pltpu.SemaphoreType.REGULAR((3,)),
+            dma((4,)), pltpu.SemaphoreType.REGULAR((2,)),
             dma((4, K)), dma((4, K)), dma((4, K)), dma((5, 3)), dma((5, 3)),
         ],
         compiler_params=pltpu.CompilerParams(collective_id=0, has_side_effects=True),

time: 68.9 us -> 66.1 us (0.959)
  Pallas kernels: 68.1 us -> 65.4 us
    pallas_call x1, Pallas kernels: 66.7 us -> 63.9 us  [on_device(): pl.pallas_call(functools.partial(kernel, scale), out_shape=tuple((pltpu.V...]
where the time goes in v5:
time: 66.1 us; the launch traced here: 66 us
  Pallas kernels  65.4 us (99%)
    pallas_call x1, Pallas kernels, on_device(): pl.pallas_call(functools.partial(kernel, scale), out_shape=tuple((pltpu.V...  63.9 us
    pallas_call x1, Pallas kernels, on_device(): pl.pallas_call(store_kernel, out_shape=tuple((jax.ShapeDtypeStruct(shape,...  1.46 us

profile of v5, /device:TPU:1, one launch (start us, length us, event | category | flops | bytes accessed | tf_op | source)
XLA Modules:
  0.0 66.0 jit_solution(14464127934622315639)
XLA Ops:
  0.6 63.9 %window.1 = (f32[2048,128]{1,0:T(8,128)S(1)}, f32[2048,128]{1,0:T(8,128)S(1)}, f32[3,256,128]{2,1,0:T(8,128)S(1)}) custom-call(f32[2048,128]{1,0:T(8,128)} %bitcast.22, f32[2048,128]{1,0:T(8,128)} %bitcast.23, f32[768,128]{1,0:T(8,128)} %bitcast.24), custom_call_target="tpu_custom_call" | custom-call | tf_op jit(solution)/shard_map/window/pallas_call | solution.py:453
  64.5 1.5 %store.1 = (f32[2048,128]{1,0:T(8,128)}, f32[2048,128]{1,0:T(8,128)}, f32[3,256,128]{2,1,0:T(8,128)}) custom-call(f32[2048,128]{1,0:T(8,128)S(1)} %get-tuple-element.9.psi_res, f32[2048,128]{1,0:T(8,128)S(1)} %get-tuple-element.10.lam_res, f32[3,256,128]{2,1,0:T(8,128)S(1)} %get-tuple-element.11.gout), custom_call_target="tpu_custom_call" | custom-call | tf_op jit(solution)/shard_map/store/pallas_call | solution.py:484

commit v6 on v5

--- a/solution.py
+++ b/solution.py
@@ -60,6 +60,7 @@
     offsets = [(dx, dz, o) for dx in range(4) for dz in range(4) for o in range(2)]
     offsets = sorted(offsets, key=lambda d: -(hops[d[0]] + hops[d[1]]))[:-2] + [(0, 0, 1)]
     same_core = [d for d in offsets if d[2] == 0]
+    bulk = sorted(offsets[:-1], key=lambda d: ((d[0] + d[1]) % 4, d[2], d[0])) + offsets[-1:]
     partner = at(0, 0, 0, 1)
 
     near = [(dy, 0, 0, 0) for dy in (2, 1, 3)]
@@ -196,7 +197,7 @@
     def tiles(ref):
         return ref.reshape(K, 4, PLANE, 8, 128)
 
-    def plane_start(st, src, dst, k, where=offsets):
+    def plane_start(st, src, dst, k, where=bulk):
         src_t, dst_t = tiles(src), tiles(dst)
         for offset in where:
             q = peer(*offset)

time: 66.1 us -> 66.4 us (level)
  no operation moved by 1% of the time
where the time goes in v6:
time: 66.4 us; the launch traced here: 66.2 us
  Pallas kernels  65.6 us (99%)
    pallas_call x1, Pallas kernels, on_device(): pl.pallas_call(functools.partial(kernel, scale), out_shape=tuple((pltpu.V...  64.1 us
    pallas_call x1, Pallas kernels, on_device(): pl.pallas_call(store_kernel, out_shape=tuple((jax.ShapeDtypeStruct(shape,...  1.46 us

profile of v6, /device:TPU:1, one launch (start us, length us, event | category | flops | bytes accessed | tf_op | source)
XLA Modules:
  0.0 66.2 jit_solution(17922619089544097481)
XLA Ops:
  0.6 64.1 %window.1 = (f32[2048,128]{1,0:T(8,128)S(1)}, f32[2048,128]{1,0:T(8,128)S(1)}, f32[3,256,128]{2,1,0:T(8,128)S(1)}) custom-call(f32[2048,128]{1,0:T(8,128)} %bitcast.22, f32[2048,128]{1,0:T(8,128)} %bitcast.23, f32[768,128]{1,0:T(8,128)} %bitcast.24), custom_call_target="tpu_custom_call" | custom-call | tf_op jit(solution)/shard_map/window/pallas_call | solution.py:454
  64.8 1.5 %store.1 = (f32[2048,128]{1,0:T(8,128)}, f32[2048,128]{1,0:T(8,128)}, f32[3,256,128]{2,1,0:T(8,128)}) custom-call(f32[2048,128]{1,0:T(8,128)S(1)} %get-tuple-element.9.psi_res, f32[2048,128]{1,0:T(8,128)S(1)} %get-tuple-element.10.lam_res, f32[3,256,128]{2,1,0:T(8,128)S(1)} %get-tuple-element.11.gout), custom_call_target="tpu_custom_call" | custom-call | tf_op jit(solution)/shard_map/store/pallas_call | solution.py:485
